TPU v7x, 128 devices: a whole 4x4x4 slice. The times are simulated.
128 devices in a mesh: ctx: 8 (over y, x_lo), tp: 16 (over x_hi, z, core).
Axes of the slice: x: 4 (x_hi: 2, x_lo: 2; x = x_hi * 2 + x_lo), y: 4, z: 4, core: 2. Of those that a mesh axis runs over, the one named last changes fastest.
Arguments:
- tokens: bfloat16 [4096, 4096], P(('ctx', 'tp')), may hold values from -16 to 16
- upstream: bfloat16 [4096, 4096], P('ctx', 'tp'), may hold values from -6 to 6
- w_query: bfloat16 [4096, 4096], P('ctx', 'tp')
- w_keyval: bfloat16 [4096, 2048], P('ctx', 'tp')
- positions: int32 [4096], replicated, may hold values from 0 to 4095, as said below
- documents: int32 [4096], replicated, may hold values from 0 to 3, never falling along the last dimension, each value on 1 to 2048 neighbouring positions
Outputs:
- token_grad: bfloat16 [4096, 4096], P(('ctx', 'tp'))
- query_grad: float32 [4096, 4096], P('ctx', 'tp')
- keyval_grad: float32 [4096, 2048], P('ctx', 'tp')
Inputs may be any that keep to these rules, and one draw needn't show every extreme that they name: Each stored run of 512 tokens holds consecutive increasing positions; the two runs of the tokens of one context rank are the blocks k and 15 - k of the sequence for some k; all runs together hold every position once.
All inputs are finite; a program needn't handle non-finite values.
Results may differ from a plain program's by a relative error of at most 0.02.
The roundings to bfloat16 on the way count: a program that leaves them out, or rounds other values in their place, can miss the bound.
Values may be sent and summed in bfloat16 or wider, within the bound.
A program may use at most 128 MiB of HBM per device.

v0:
```python
import jax
import jax.numpy as jnp
from jax import lax
from jax.sharding import PartitionSpec as P

KEY_VALUE_HEADS = 8
HEAD_DIMENSION = 128
rope_base = 500000.0


def side_by_side(arrays, axis, dim, along):
    both = jnp.concatenate(arrays, axis=along)
    filled, at, gathered = (lax.all_gather(both, axis, axis=dim, tiled=True), 0, [])
    for a in arrays:
        gathered.append(lax.slice_in_dim(filled, at, at + a.shape[along], axis=along))
        at += a.shape[along]
    return tuple(gathered)


def partner_2(block, axis, bit):
    count = lax.axis_size(axis)
    route = []
    for low in range(count):
        high = low | 1 << bit
        if high != low and high < count:
            route += [(low, high), (high, low)]
    return lax.ppermute(block, axis, route)


def copy_for_each(x, axis):
    count = lax.axis_size(axis)
    return lax.all_to_all(jnp.broadcast_to(x[None], (count, *x.shape)), axis, 0, 0, tiled=True)


def laid_out(blocks, dim):
    lengths = list(blocks.shape[1:])
    lengths[dim] *= blocks.shape[0]
    return jnp.moveaxis(blocks, 0, dim).reshape(lengths)


def gathered_copies(x, axis, dim):
    blocks = copy_for_each(x, axis)
    return laid_out(blocks, dim)


def cut_along(x, dim, count):
    lengths = x.shape
    blocks = x.reshape(*lengths[:dim], count, lengths[dim] // count, *lengths[dim + 1 :])
    return jnp.moveaxis(blocks, dim, 0)


def summed_on_arrival(x, axis, dim):
    count = lax.axis_size(axis)
    blocks = lax.all_to_all(cut_along(x, dim, count), axis, 0, 0, tiled=True)
    return jnp.sum(blocks.astype(jnp.float32), axis=0)


def rotation_tables(positions):
    half_width = HEAD_DIMENSION // 2
    frequency = rope_base ** (-(jnp.arange(half_width, dtype=jnp.float32) * 2.0 / HEAD_DIMENSION))
    angles = positions.astype(jnp.float32)[:, None] * frequency[None, :]
    cosine = jnp.concatenate([jnp.cos(angles), jnp.cos(angles)], axis=1)
    sine = jnp.concatenate([jnp.sin(angles), jnp.sin(angles)], axis=1)
    return (cosine, sine)


def rotate(values, cosine, sine):
    half_width = values.shape[-1] // 2
    turned = jnp.concatenate([-values[..., half_width:], values[..., :half_width]], axis=-1)
    return values * cosine[:, None, :] + turned * sine[:, None, :]


def rotate_back(gradient, cosine, sine):
    half_width = gradient.shape[-1] // 2
    scaled = gradient * sine[:, None, :]
    turned = jnp.concatenate([scaled[..., half_width:], -scaled[..., :half_width]], axis=-1)
    return gradient * cosine[:, None, :] + turned


def attend(
    query_rows, grad_out, keys_all, values_all, query_pos, query_doc, key_pos, key_doc, scaling
):
    f32 = jnp.float32
    tok_rows, head_count, head_width = query_rows.shape
    block_rows = min(tok_rows, 128)
    block_count = tok_rows // block_rows
    seq_len = keys_all.shape[0]

    def advance(totals, inputs):
        key_total, value_total = totals
        query_block, grad_block, pos_block, doc_block = inputs
        scores = (
            jnp.einsum("qhd,kd->hqk", query_block, keys_all, preferred_element_type=f32) * scaling
        )
        visible = (key_pos[None, :] <= pos_block[:, None]) & (
            key_doc[None, :] == doc_block[:, None]
        )
        scores = jnp.where(visible[None], scores, -1e30)
        row_peak = jnp.max(scores, axis=-1, keepdims=True)
        exponent = jnp.exp(scores - row_peak)
        probs = exponent / jnp.sum(exponent, axis=-1, keepdims=True)
        probs_half = probs.astype(jnp.bfloat16)
        output = jnp.einsum("hqk,kd->qhd", probs_half, values_all, preferred_element_type=f32)
        deltas = jnp.sum(grad_block.astype(f32) * output, axis=-1)
        prob_grad = jnp.einsum("qhd,kd->hqk", grad_block, values_all, preferred_element_type=f32)
        score_grad = (probs * (prob_grad - deltas.T[:, :, None])).astype(jnp.bfloat16)
        dquery = (
            jnp.einsum("hqk,kd->qhd", score_grad, keys_all, preferred_element_type=f32) * scaling
        )
        key_total = (
            key_total
            + jnp.einsum("hqk,qhd->kd", score_grad, query_block, preferred_element_type=f32)
            * scaling
        )
        value_total = value_total + jnp.einsum(
            "hqk,qhd->kd", probs_half, grad_block, preferred_element_type=f32
        )
        return ((key_total, value_total), dquery)

    blank_keys = jnp.zeros((seq_len, head_width), f32)
    inputs = (
        query_rows.reshape(block_count, block_rows, head_count, head_width),
        grad_out.reshape(block_count, block_rows, head_count, head_width),
        query_pos.reshape(block_count, block_rows),
        query_doc.reshape(block_count, block_rows),
    )
    (key_total, value_total), dquery = lax.scan(advance, (blank_keys, blank_keys), inputs)
    return (dquery.reshape(tok_rows, head_count, head_width), key_total, value_total)


def shards(tokens, upstream, w_query, w_keyval, positions, documents):
    f32 = jnp.float32
    ctx_rank = lax.axis_index("ctx")
    tp_rank = lax.axis_index("tp")
    tensor_split_count = lax.axis_size("tp")
    gathered = lax.all_gather(tokens, "tp", axis=0, tiled=True)
    tok_rows = gathered.shape[0]
    query_cols = w_query.shape[1]
    head_count = query_cols // HEAD_DIMENSION
    pairing_flags = (tensor_split_count // KEY_VALUE_HEADS).bit_length() - 1
    doc_all = jnp.take(documents, positions)
    cosine_all, sine_all = rotation_tables(positions)
    row_offset = ctx_rank * tok_rows
    my_pos = lax.dynamic_slice_in_dim(positions, row_offset, tok_rows, 0)
    my_doc = lax.dynamic_slice_in_dim(doc_all, row_offset, tok_rows, 0)
    my_cos = lax.dynamic_slice_in_dim(cosine_all, row_offset, tok_rows, 0)
    my_sin = lax.dynamic_slice_in_dim(sine_all, row_offset, tok_rows, 0)
    query_full, keyval_full = side_by_side((w_query, w_keyval), "ctx", 0, 1)
    query_raw = jnp.dot(gathered, query_full, preferred_element_type=f32)
    keyval_raw = jnp.dot(gathered, keyval_full, preferred_element_type=f32)
    query_rot = rotate(
        query_raw.reshape(tok_rows, head_count, HEAD_DIMENSION), my_cos, my_sin
    ).astype(jnp.bfloat16)
    head_kv = keyval_raw.astype(jnp.bfloat16)
    bit_index = 0
    partner = partner_2(head_kv, "tp", bit_index)
    is_lower = tp_rank // (1 << bit_index) % 2 == 0
    head_kv = jnp.where(
        is_lower,
        jnp.concatenate([head_kv, partner], axis=1),
        jnp.concatenate([partner, head_kv], axis=1),
    )
    key_rot = rotate(head_kv[:, None, :HEAD_DIMENSION].astype(f32), my_cos, my_sin)[:, 0].astype(
        jnp.bfloat16
    )
    local_kv = jnp.concatenate([key_rot, head_kv[:, HEAD_DIMENSION:]], axis=1)
    key_value = gathered_copies(local_kv, "ctx", 0)
    grad_query, grad_key, grad_value = attend(
        query_rot,
        upstream.reshape(tok_rows, head_count, HEAD_DIMENSION),
        key_value[:, :HEAD_DIMENSION],
        key_value[:, HEAD_DIMENSION:],
        my_pos,
        my_doc,
        positions,
        doc_all,
        HEAD_DIMENSION ** (-0.5),
    )
    query_back = (
        rotate_back(grad_query, my_cos, my_sin).astype(jnp.bfloat16).reshape(tok_rows, query_cols)
    )
    key_backward = rotate_back(grad_key[:, None, :], cosine_all, sine_all)[:, 0]
    key_terms = jnp.concatenate([key_backward, grad_value], axis=1)
    head_grad = summed_on_arrival(key_terms.astype(jnp.bfloat16), "ctx", 0)
    for bit_index in reversed(range(pairing_flags)):
        half_width = head_grad.shape[1] // 2
        lower_half = head_grad[:, :half_width]
        upper_half = head_grad[:, half_width:]
        is_lower = tp_rank // (1 << bit_index) % 2 == 0
        retained = jnp.where(is_lower, lower_half, upper_half)
        outgoing = jnp.where(is_lower, upper_half, lower_half)
        head_grad = retained + partner_2(outgoing.astype(jnp.bfloat16), "tp", bit_index).astype(
            outgoing.dtype
        )
    key_value_backward = head_grad.astype(jnp.bfloat16)
    row_grads = jnp.concatenate([query_back, key_value_backward], axis=1)
    part_query = lax.dot_general(
        row_grads[:, :query_cols], query_full, (((1,), (1,)), ((), ())), preferred_element_type=f32
    )
    part_keyval = lax.dot_general(
        row_grads[:, query_cols:], keyval_full, (((1,), (1,)), ((), ())), preferred_element_type=f32
    )
    token_grad = lax.psum_scatter(
        (part_query + part_keyval).astype(jnp.bfloat16), "tp", scatter_dimension=0, tiled=True
    )
    weight_grad = summed_on_arrival(
        lax.dot_general(
            gathered, row_grads, (((0,), (0,)), ((), ())), preferred_element_type=f32
        ).astype(jnp.bfloat16),
        "ctx",
        0,
    )
    return (token_grad, weight_grad[:, :query_cols], weight_grad[:, query_cols:])


def solution(mesh):
    return jax.shard_map(
        shards,
        mesh=mesh,
        in_specs=(P(("ctx", "tp"), None), P("ctx", "tp"), P("ctx", "tp"), P("ctx", "tp"), P(), P()),
        out_specs=(P(("ctx", "tp"), None), P("ctx", "tp"), P("ctx", "tp")),
        check_vma=False,
    )
```

profile of v0, /device:TPU:0, one launch (start us, length us, event | category | flops | bytes accessed | tf_op | source)
XLA Modules:
  0.0 420.5 jit_solution(1429676096698661029)
XLA Ops:
  10.5 23.0 %gather_fusion = s32[4096]{0:T(1024)S(1)} fusion(s32[4096]{0:T(1024)S(1)} %copy-done, s32[4096]{0:T(1024)S(1)} %fusion.68), kind=kCustom, calls=%fused_computation | custom fusion | bytes 49152 | tf_op jit(solution)/shard_map/jit(_take)/gather | solution.py:141
  33.6 50.6 %all-gather.3.cloned.1.call-done = bf16[4096,384]{1,0:T(8,128)(2,1)} async-done(((bf16[512,384]{1,0:T(8,128)(2,1)}), bf16[4096,384]{1,0:T(8,128)(2,1)}) %all-gather.3.cloned.1.call-update) | async-done | bytes 3145744 | tf_op jit(solution)/shard_map/all_gather | solution.py:13
  84.2 57.0 %all-gather.5.cloned.1.call-done = bf16[512,4096]{1,0:T(8,128)(2,1)} async-done(((bf16[32,4096]{1,0:T(8,128)(2,1)}), bf16[512,4096]{1,0:T(8,128)(2,1)}) %all-gather.5.cloned.1.call-update) | async-done | bytes 4194320 | tf_op jit(solution)/shard_map/all_gather | solution.py:136
  141.2 4.0 fusion.52
  145.5 3.7 multiply_cosine_fusion
  152.2 4.4 %all-to-all-start = ((bf16[8,512,256]{1,2,0:T(8,128)(2,1)}), bf16[8,512,256]{1,2,0:T(8,128)(2,1)S(1)}, u32[]{:S(2)}, u32[]{:S(2)}) async-start(bf16[8,512,256]{1,2,0:T(8,128)(2,1)} %broadcast_in_dim.33), calls=%async_computation | async-start | bytes 4194304 | tf_op jit(solution)/shard_map/all_to_all | solution.py:32
  157.5 4.1 fusion.50
  171.2 12.9 %all-to-all-done = bf16[8,512,256]{1,2,0:T(8,128)(2,1)S(1)} async-done(((bf16[8,512,256]{1,2,0:T(8,128)(2,1)}), bf16[8,512,256]{1,2,0:T(8,128)(2,1)S(1)}, u32[]{:S(2)}, u32[]{:S(2)}) %all-to-all-start) | async-done | bytes 2097184 | tf_op jit(solution)/shard_map/all_to_all | solution.py:32
  189.6 89.4 %while.15 = (s32[]{:T(128)}, f32[4096,128]{1,0:T(8,128)}, f32[4096,128]{1,0:T(8,128)}, f32[4,128,2,128]{3,1,2,0:T(8,128)}, s32[4096]{0:T(1024)S(1)}, /*index=5*/...) while((s32[]{:T(128)}, f32[4096,128]{1,0:T(8,128)}, ...), condition=%wide.region_4.5_spmd.clone, body=%wide.region_0.4_spmd.clone.sunk | while | flops 1625427712 | bytes 64595660 | solution.py:127
  190.1 4.9 %fusion.118 = (f32[2,128]{1,0:T(2,128)S(1)}, f32[2,128,4096]{2,1,0:T(8,128)}) fusion(pred[128,4096]{1,0:T(8,128)(4,1)S(1)} %compare_and_fusion.2, bf16[4096,128]{1,0:T(8,128)(2,1)} %get-tuple-element.330, bf16[4,128,2,128]{3,1,2,0:T(8,128)(2,1)} %get-tuple-element.329, s32[]{:T(128)} %get-tuple-element.307), kind=kOutput, calls=%fused_computation.112.clone.1 | convolution fusion | flops 272633856 | bytes 5834240 | tf_op jit(solution)/shard_map/while/body/eval_jaxpr/sub | solution.py:100
  201.6 4.0 fusion.122
  210.8 4.9 %fusion.118 = (f32[2,128]{1,0:T(2,128)S(1)}, f32[2,128,4096]{2,1,0:T(8,128)}) fusion(pred[128,4096]{1,0:T(8,128)(4,1)S(1)} %compare_and_fusion.2, bf16[4096,128]{1,0:T(8,128)(2,1)} %get-tuple-element.330, bf16[4,128,2,128]{3,1,2,0:T(8,128)(2,1)} %get-tuple-element.329, s32[]{:T(128)} %get-tuple-element.307), kind=kOutput, calls=%fused_computation.112.clone.1 | convolution fusion | flops 272633856 | bytes 5834240 | tf_op jit(solution)/shard_map/while/body/eval_jaxpr/sub | solution.py:100
  222.3 4.6 %fusion.122 = f32[4096,128]{1,0:T(8,128)} fusion(bf16[2,128,4096]{2,1,0:T(8,128)(2,1)} %fusion.121, f32[4096,128]{1,0:T(8,128)} %get-tuple-element.308, pred[]{:T(512)S(6)} %compare.5, bf16[4,128,2,128]{3,1,2,0:T(8,128)(2,1)} %get-tuple-element.329, s32[]{:T(128)} %get-tuple-element.307), kind=kOutput, calls=%fused_computation.14.clone.1 | convolution fusion | flops 270008320 | bytes 6357505 | tf_op jit(solution)/shard_map/while/body/eval_jaxpr/hqk,qhd->kd/dot_general | solution.py:112
  233.7 4.9 %fusion.118 = (f32[2,128]{1,0:T(2,128)S(1)}, f32[2,128,4096]{2,1,0:T(8,128)}) fusion(pred[128,4096]{1,0:T(8,128)(4,1)S(1)} %compare_and_fusion.2, bf16[4096,128]{1,0:T(8,128)(2,1)} %get-tuple-element.330, bf16[4,128,2,128]{3,1,2,0:T(8,128)(2,1)} %get-tuple-element.329, s32[]{:T(128)} %get-tuple-element.307), kind=kOutput, calls=%fused_computation.112.clone.1 | convolution fusion | flops 272633856 | bytes 5834240 | tf_op jit(solution)/shard_map/while/body/eval_jaxpr/sub | solution.py:100
  245.2 4.6 %fusion.122 = f32[4096,128]{1,0:T(8,128)} fusion(bf16[2,128,4096]{2,1,0:T(8,128)(2,1)} %fusion.121, f32[4096,128]{1,0:T(8,128)} %get-tuple-element.308, pred[]{:T(512)S(6)} %compare.5, bf16[4,128,2,128]{3,1,2,0:T(8,128)(2,1)} %get-tuple-element.329, s32[]{:T(128)} %get-tuple-element.307), kind=kOutput, calls=%fused_computation.14.clone.1 | convolution fusion | flops 270008320 | bytes 6357505 | tf_op jit(solution)/shard_map/while/body/eval_jaxpr/hqk,qhd->kd/dot_general | solution.py:112
  252.4 3.7 fusion.123
  256.6 4.9 %fusion.118 = (f32[2,128]{1,0:T(2,128)S(1)}, f32[2,128,4096]{2,1,0:T(8,128)}) fusion(pred[128,4096]{1,0:T(8,128)(4,1)S(1)} %compare_and_fusion.2, bf16[4096,128]{1,0:T(8,128)(2,1)} %get-tuple-element.330, bf16[4,128,2,128]{3,1,2,0:T(8,128)(2,1)} %get-tuple-element.329, s32[]{:T(128)} %get-tuple-element.307), kind=kOutput, calls=%fused_computation.112.clone.1 | convolution fusion | flops 272633856 | bytes 5834240 | tf_op jit(solution)/shard_map/while/body/eval_jaxpr/sub | solution.py:100
  268.1 4.6 %fusion.122 = f32[4096,128]{1,0:T(8,128)} fusion(bf16[2,128,4096]{2,1,0:T(8,128)(2,1)} %fusion.121, f32[4096,128]{1,0:T(8,128)} %get-tuple-element.308, pred[]{:T(512)S(6)} %compare.5, bf16[4,128,2,128]{3,1,2,0:T(8,128)(2,1)} %get-tuple-element.329, s32[]{:T(128)} %get-tuple-element.307), kind=kOutput, calls=%fused_computation.14.clone.1 | convolution fusion | flops 270008320 | bytes 6357505 | tf_op jit(solution)/shard_map/while/body/eval_jaxpr/hqk,qhd->kd/dot_general | solution.py:112
  288.7 3.7 all-to-all-start.1
  294.0 24.9 %all-to-all-done.1 = bf16[8,512,256]{1,2,0:T(8,128)(2,1)S(1)} async-done(((bf16[8,512,256]{1,2,0:T(8,128)(2,1)}), bf16[8,512,256]{1,2,0:T(8,128)(2,1)S(1)}, u32[]{:S(2)}, u32[]{:S(2)}) %all-to-all-start.1) | async-done | bytes 2097184 | tf_op jit(solution)/shard_map/all_to_all | solution.py:54
  322.3 4.5 %add_convert_fusion = bf16[512,4096]{1,0:T(8,128)(2,1)} fusion(f32[512,4096]{1,0:T(8,128)S(1)} %fusion.48, bf16[512,128]{0,1:T(8,128)(2,1)S(1)} %add_convert_fusion.1, bf16[4096,384]{1,0:T(8,128)(2,1)} %all-gather.3.cloned.1.call-done), kind=kOutput, calls=%fused_computation.47 | convolution fusion | flops 541065216 | bytes 13762560 | tf_op jit(solution)/shard_map/dot_general | solution.py:200
  327.0 4.0 convolution_convert_fusion
  331.3 52.4 %all_to_all.15 = bf16[8,512,384]{1,2,0:T(8,128)(2,1)S(1)} all-to-all(bf16[8,512,384]{1,2,0:T(8,128)(2,1)S(1)} %bitcast.184), channel_id=1, replica_groups=mesh['ctx'=8,'tp'=16] {'ctx'}, dimensions={0} | all-to-all | bytes 6291456 | tf_op jit(solution)/shard_map/all_to_all | solution.py:54
  386.0 27.9 %reduce-scatter.2.cloned.1.call-done = bf16[32,4096]{1,0:T(8,128)(2,1)} async-done(((bf16[512,4096]{1,0:T(8,128)(2,1)}), bf16[32,4096]{1,0:T(8,128)(2,1)}) %reduce-scatter.2.cloned.1.call-update) | async-done | bytes 262160 | tf_op jit(solution)/shard_map/reduce_scatter | solution.py:203
  (136 shorter events, 88.0 us)
Async XLA Ops:
  7.2 3.4 copy-start
  7.2 77.0 %all-gather.3.cloned.1.call-start = ((), (), s32[]{:S(2)}) async-start(), calls=%async_computation.4 | async-start | bytes 3538944 | tf_op jit(solution)/shard_map/all_gather | solution.py:13
  9.1 132.1 %all-gather.5.cloned.1.call-start = ((), (), s32[]{:S(2)}) async-start(), calls=%async_computation.5 | async-start | bytes 4456448 | tf_op jit(solution)/shard_map/all_gather | solution.py:136
  10.5 23.1 %copy-start.13 = (s32[4096]{0:T(1024)S(1)}, s32[4096]{0:T(1024)}, u32[]{:S(2)}) copy-start(s32[4096]{0:T(1024)} %param.12) | copy-start | bytes 49156
  145.2 4.1 collective-permute-start
  152.2 4.5 %copy-start.14 = (bf16[512,256]{1,0:T(8,128)(2,1)S(1)}, bf16[512,256]{1,0:T(8,128)(2,1)}, u32[]{:S(2)}) copy-start(bf16[512,256]{1,0:T(8,128)(2,1)} %param.9) | copy-start | bytes 786436
  152.2 31.8 %all-to-all-start = ((bf16[8,512,256]{1,2,0:T(8,128)(2,1)}), bf16[8,512,256]{1,2,0:T(8,128)(2,1)S(1)}, u32[]{:S(2)}, u32[]{:S(2)}) async-start(bf16[8,512,256]{1,2,0:T(8,128)(2,1)} %broadcast_in_dim.33), calls=%async_computation | async-start | bytes 4194304 | tf_op jit(solution)/shard_map/all_to_all | solution.py:32
  163.5 3.9 copy-start.12
  166.5 19.9 %copy-start.9 = (f32[512,128]{1,0:T(8,128)}, f32[512,128]{1,0:T(8,128)S(1)}, u32[]{:S(2)}) copy-start(f32[512,128]{1,0:T(8,128)S(1)} %copy.70) | copy-start | bytes 786436
  195.1 4.5 %copy-start.3 = (f32[2,128,4096]{2,1,0:T(8,128)S(1)}, f32[2,128,4096]{2,1,0:T(8,128)}, u32[]{:S(2)}) copy-start(f32[2,128,4096]{2,1,0:T(8,128)} %get-tuple-element.291) | copy-start | bytes 12582916 | tf_op jit(solution)/shard_map/while
  201.6 4.0 copy-start.2
  215.7 4.5 %copy-start.3 = (f32[2,128,4096]{2,1,0:T(8,128)S(1)}, f32[2,128,4096]{2,1,0:T(8,128)}, u32[]{:S(2)}) copy-start(f32[2,128,4096]{2,1,0:T(8,128)} %get-tuple-element.291) | copy-start | bytes 12582916 | tf_op jit(solution)/shard_map/while
  222.3 4.6 %copy-start.2 = (bf16[2,128,4096]{2,1,0:T(8,128)(2,1)S(1)}, bf16[2,128,4096]{2,1,0:T(8,128)(2,1)}, u32[]{:S(2)}) copy-start(bf16[2,128,4096]{2,1,0:T(8,128)(2,1)} %fusion.121) | copy-start | bytes 6291460 | tf_op jit(solution)/shard_map/while
  238.6 4.5 %copy-start.3 = (f32[2,128,4096]{2,1,0:T(8,128)S(1)}, f32[2,128,4096]{2,1,0:T(8,128)}, u32[]{:S(2)}) copy-start(f32[2,128,4096]{2,1,0:T(8,128)} %get-tuple-element.291) | copy-start | bytes 12582916 | tf_op jit(solution)/shard_map/while
  245.2 4.6 %copy-start.2 = (bf16[2,128,4096]{2,1,0:T(8,128)(2,1)S(1)}, bf16[2,128,4096]{2,1,0:T(8,128)(2,1)}, u32[]{:S(2)}) copy-start(bf16[2,128,4096]{2,1,0:T(8,128)(2,1)} %fusion.121) | copy-start | bytes 6291460 | tf_op jit(solution)/shard_map/while
  261.5 4.5 %copy-start.3 = (f32[2,128,4096]{2,1,0:T(8,128)S(1)}, f32[2,128,4096]{2,1,0:T(8,128)}, u32[]{:S(2)}) copy-start(f32[2,128,4096]{2,1,0:T(8,128)} %get-tuple-element.291) | copy-start | bytes 12582916 | tf_op jit(solution)/shard_map/while
  268.1 4.6 %copy-start.2 = (bf16[2,128,4096]{2,1,0:T(8,128)(2,1)S(1)}, bf16[2,128,4096]{2,1,0:T(8,128)(2,1)}, u32[]{:S(2)}) copy-start(bf16[2,128,4096]{2,1,0:T(8,128)(2,1)} %fusion.121) | copy-start | bytes 6291460 | tf_op jit(solution)/shard_map/while
  279.0 2.0 copy-start.5
  284.2 1.9 copy-start.8
  288.7 4.0 copy-start.11
  288.7 30.2 %all-to-all-start.1 = ((bf16[8,512,256]{1,2,0:T(8,128)(2,1)}), bf16[8,512,256]{1,2,0:T(8,128)(2,1)S(1)}, u32[]{:S(2)}, u32[]{:S(2)}) async-start(bf16[8,512,256]{1,2,0:T(8,128)(2,1)} %copy.84), calls=%async_computation.1 | async-start | bytes 4194304 | tf_op jit(solution)/shard_map/all_to_all | solution.py:54
  292.4 121.5 %reduce-scatter.2.cloned.1.call-start = ((), (), s32[]{:S(2)}) async-start(), calls=%async_computation.6 | async-start | bytes 4456448 | tf_op jit(solution)/shard_map/reduce_scatter | solution.py:203
  319.2 3.0 collective-permute-start.1
  383.6 30.3 %copy-start.1 = (s32[4096]{0:T(1024)S(1)}, s32[4096]{0:T(1024)}, u32[]{:S(2)}) copy-start(s32[4096]{0:T(1024)} %param.13) | copy-start | bytes 49156
  (4 other events, 4.9 us)
Sparse Core Ops, SparseCore 0:
  10.2 73.9 all-gather.2
  86.7 54.4 all-gather.4
  327.0 86.9 reduce-scatter.1
where the time goes:
time: 422 us; the launch traced here: 420 us
  waiting for transfers between devices  174 us (41%)
  matrix products  92 us (22%)
  blocking collectives  52.4 us (12%)
  local copies, waits for them, and re-layouts  52.2 us (12%)
  other arithmetic  26.7 us (6%)
  between operations  14.2 us (3%)
  starting transfers between devices  8.92 us (2%)
    all_gather x1, waiting for transfers between devices, shards(): gathered = lax.all_gather(tokens, 'tp', axis=0, tiled=True)  57 us
    all_to_all x1, blocking collectives, summed_on_arrival(): blocks = lax.all_to_all(cut_along(x, dim, count), axis, 0, 0, tiled=True)  52.4 us
    all_gather x1, waiting for transfers between devices, side_by_side(): lax.all_gather(both, axis, axis=dim, tiled=True)  50.6 us
    reduce_scatter x1, waiting for transfers between devices, shards(): lax.psum_scatter((part_query + part_keyval).astype(jnp.bfloat16), 'tp', s...  27.9 us
    all_to_all x1, waiting for transfers between devices, summed_on_arrival(): blocks = lax.all_to_all(cut_along(x, dim, count), axis, 0, 0, tiled=True)  24.9 us
    gather x1, local copies, waits for them, and re-layouts, shards(): doc_all = jnp.take(documents, positions)  23 us
    sub x4, matrix products, advance(): exponent = jnp.exp(scores - row_peak)  19.7 us
    dot_general x4, matrix products, advance(): jnp.einsum('hqk,qhd->kd', score_grad, query_block, preferred_element_type...  17.7 us
  transfers between devices with their start and end apart: 7, of which 5 were waited for; matrix products, arithmetic and copies ran while one was open for 13% of the time, Pallas kernels for 0%

commit v1 on v0

--- a/solution.py
+++ b/solution.py
@@ -133,7 +133,9 @@
     ctx_rank = lax.axis_index("ctx")
     tp_rank = lax.axis_index("tp")
     tensor_split_count = lax.axis_size("tp")
-    gathered = lax.all_gather(tokens, "tp", axis=0, tiled=True)
+    gathered = jnp.concatenate(
+        lax.all_to_all(jnp.stack([tokens] * lax.axis_size("tp")), "tp", 0, 0), axis=0
+    )
     tok_rows = gathered.shape[0]
     query_cols = w_query.shape[1]
     head_count = query_cols // HEAD_DIMENSION

time: 422 us -> 411 us (0.974)
  waiting for transfers between devices: 174 us -> 155 us
  starting transfers between devices: 8.92 us -> 16.4 us
    all_to_all x0 -> x1, waiting for transfers between devices: none -> 73.7 us  [shards(): lax.all_to_all(jnp.stack([tokens] * lax.axis_size('tp')), 'tp', 0, 0)]
    all_gather x1 -> x0, waiting for transfers between devices: 57 us -> none  [shards(): gathered = lax.all_gather(tokens, 'tp', axis=0, tiled=True)]
    all_gather x1, waiting for transfers between devices: 50.6 us -> 11.2 us  [side_by_side(): lax.all_gather(both, axis, axis=dim, tiled=True)]
    all_to_all x0 -> x1, starting transfers between devices: none -> 8.17 us  [shards(): lax.all_to_all(jnp.stack([tokens] * lax.axis_size('tp')), 'tp', 0, 0)]
    reduce_scatter x1, waiting for transfers between devices: 27.9 us -> 32.2 us  [shards(): lax.psum_scatter((part_query + part_keyval).astype(jnp.bfloat16), 'tp', s...]
  transfers between devices with their start and end apart: 7 -> 7, of which waited for: 5 -> 5; matrix products, arithmetic and copies ran while one was open for 13% -> 14% of each run, Pallas kernels for 0% -> 0%
where the time goes in v1:
time: 411 us; the launch traced here: 409 us
  waiting for transfers between devices  155 us (38%)
  matrix products  91.9 us (22%)
  local copies, waits for them, and re-layouts  55.6 us (14%)
  blocking collectives  49.5 us (12%)
  other arithmetic  26 us (6%)
  starting transfers between devices  16.4 us (4%)
  between operations  14.5 us (4%)
    all_to_all x1, waiting for transfers between devices, shards(): lax.all_to_all(jnp.stack([tokens] * lax.axis_size('tp')), 'tp', 0, 0)  73.7 us
    all_to_all x1, blocking collectives, summed_on_arrival(): blocks = lax.all_to_all(cut_along(x, dim, count), axis, 0, 0, tiled=True)  49.5 us
    reduce_scatter x1, waiting for transfers between devices, shards(): lax.psum_scatter((part_query + part_keyval).astype(jnp.bfloat16), 'tp', s...  32.2 us
    all_to_all x1, waiting for transfers between devices, summed_on_arrival(): blocks = lax.all_to_all(cut_along(x, dim, count), axis, 0, 0, tiled=True)  25.1 us
    gather x1, local copies, waits for them, and re-layouts, shards(): doc_all = jnp.take(documents, positions)  23 us
    sub x4, matrix products, advance(): exponent = jnp.exp(scores - row_peak)  19.6 us
    dot_general x4, matrix products, advance(): jnp.einsum('hqk,qhd->kd', score_grad, query_block, preferred_element_type...  17.8 us
    all_to_all x1, waiting for transfers between devices, copy_for_each(): lax.all_to_all(jnp.broadcast_to(x[None], (count, *x.shape)), axis, 0, 0,...  13.1 us
  transfers between devices with their start and end apart: 7, of which 5 were waited for; matrix products, arithmetic and copies ran while one was open for 14% of the time, Pallas kernels for 0%

profile of v1, /device:TPU:0, one launch (start us, length us, event | category | flops | bytes accessed | tf_op | source)
XLA Modules:
  0.0 409.4 jit_solution(15835393459151553913)
XLA Ops:
  12.5 8.2 %all-to-all-start = ((bf16[16,32,4096]{2,1,0:T(8,128)(2,1)}), bf16[16,32,4096]{2,1,0:T(8,128)(2,1)}, u32[]{:S(2)}, u32[]{:S(2)}) async-start(bf16[16,32,4096]{2,1,0:T(8,128)(2,1)} %stack.2), calls=%async_computation | async-start | bytes 8388608 | tf_op jit(solution)/shard_map/all_to_all | solution.py:137
  20.7 23.0 %gather_fusion = s32[4096]{0:T(1024)S(1)} fusion(s32[4096]{0:T(1024)S(1)} %copy-done, s32[4096]{0:T(1024)S(1)} %fusion.68), kind=kCustom, calls=%fused_computation | custom fusion | bytes 49152 | tf_op jit(solution)/shard_map/jit(_take)/gather | solution.py:143
  43.8 73.7 %all-to-all-done = bf16[16,32,4096]{2,1,0:T(8,128)(2,1)} async-done(((bf16[16,32,4096]{2,1,0:T(8,128)(2,1)}), bf16[16,32,4096]{2,1,0:T(8,128)(2,1)}, u32[]{:S(2)}, u32[]{:S(2)}) %all-to-all-start) | async-done | bytes 4194336 | tf_op jit(solution)/shard_map/all_to_all | solution.py:137
  117.5 11.2 %all-gather.2.cloned.1.call-done = bf16[4096,384]{1,0:T(8,128)(2,1)} async-done(((bf16[512,384]{1,0:T(8,128)(2,1)}), bf16[4096,384]{1,0:T(8,128)(2,1)}) %all-gather.2.cloned.1.call-update) | async-done | bytes 3145744 | tf_op jit(solution)/shard_map/all_gather | solution.py:13
  128.7 4.0 fusion.52
  132.8 3.7 multiply_cosine_fusion
  139.5 4.0 all-to-all-start.1
  144.4 4.1 %fusion.50 = f32[256,512]{1,0:T(8,128)S(1)} fusion(bf16[512,4096]{1,0:T(8,128)(2,1)} %bitcast.2, bf16[4096,384]{1,0:T(8,128)(2,1)} %all-gather.2.cloned.1.call-done), kind=kOutput, calls=%fused_computation.66 | convolution fusion | flops 1073741824 | bytes 6815744 | tf_op jit(solution)/shard_map/dot_general | solution.py:151
  158.1 13.1 %all-to-all-done.1 = bf16[8,512,256]{1,2,0:T(8,128)(2,1)S(1)} async-done(((bf16[8,512,256]{1,2,0:T(8,128)(2,1)}), bf16[8,512,256]{1,2,0:T(8,128)(2,1)S(1)}, u32[]{:S(2)}, u32[]{:S(2)}) %all-to-all-start.1) | async-done | bytes 2097184 | tf_op jit(solution)/shard_map/all_to_all | solution.py:32
  176.7 89.3 %while.15 = (s32[]{:T(128)}, f32[4096,128]{1,0:T(8,128)}, f32[4096,128]{1,0:T(8,128)}, f32[4,128,2,128]{3,1,2,0:T(8,128)}, s32[4096]{0:T(1024)S(1)}, /*index=5*/...) while((s32[]{:T(128)}, f32[4096,128]{1,0:T(8,128)}, ...), condition=%wide.region_4.5_spmd.clone, body=%wide.region_0.4_spmd.clone.sunk | while | flops 1625427712 | bytes 64595660 | solution.py:127
  177.2 4.9 %fusion.118 = (f32[2,128]{1,0:T(2,128)S(1)}, f32[2,128,4096]{2,1,0:T(8,128)}) fusion(pred[128,4096]{1,0:T(8,128)(4,1)S(1)} %compare_and_fusion.2, bf16[4096,128]{1,0:T(8,128)(2,1)} %get-tuple-element.330, bf16[4,128,2,128]{3,1,2,0:T(8,128)(2,1)} %get-tuple-element.329, s32[]{:T(128)} %get-tuple-element.307), kind=kOutput, calls=%fused_computation.112.clone.1 | convolution fusion | flops 272633856 | bytes 5834240 | tf_op jit(solution)/shard_map/while/body/eval_jaxpr/sub | solution.py:100
  188.7 4.0 fusion.122
  197.9 4.9 %fusion.118 = (f32[2,128]{1,0:T(2,128)S(1)}, f32[2,128,4096]{2,1,0:T(8,128)}) fusion(pred[128,4096]{1,0:T(8,128)(4,1)S(1)} %compare_and_fusion.2, bf16[4096,128]{1,0:T(8,128)(2,1)} %get-tuple-element.330, bf16[4,128,2,128]{3,1,2,0:T(8,128)(2,1)} %get-tuple-element.329, s32[]{:T(128)} %get-tuple-element.307), kind=kOutput, calls=%fused_computation.112.clone.1 | convolution fusion | flops 272633856 | bytes 5834240 | tf_op jit(solution)/shard_map/while/body/eval_jaxpr/sub | solution.py:100
  209.4 4.6 %fusion.122 = f32[4096,128]{1,0:T(8,128)} fusion(bf16[2,128,4096]{2,1,0:T(8,128)(2,1)} %fusion.121, f32[4096,128]{1,0:T(8,128)} %get-tuple-element.308, pred[]{:T(512)S(6)} %compare.5, bf16[4,128,2,128]{3,1,2,0:T(8,128)(2,1)} %get-tuple-element.329, s32[]{:T(128)} %get-tuple-element.307), kind=kOutput, calls=%fused_computation.14.clone.1 | convolution fusion | flops 270008320 | bytes 6357505 | tf_op jit(solution)/shard_map/while/body/eval_jaxpr/hqk,qhd->kd/dot_general | solution.py:112
  220.7 4.9 %fusion.118 = (f32[2,128]{1,0:T(2,128)S(1)}, f32[2,128,4096]{2,1,0:T(8,128)}) fusion(pred[128,4096]{1,0:T(8,128)(4,1)S(1)} %compare_and_fusion.2, bf16[4096,128]{1,0:T(8,128)(2,1)} %get-tuple-element.330, bf16[4,128,2,128]{3,1,2,0:T(8,128)(2,1)} %get-tuple-element.329, s32[]{:T(128)} %get-tuple-element.307), kind=kOutput, calls=%fused_computation.112.clone.1 | convolution fusion | flops 272633856 | bytes 5834240 | tf_op jit(solution)/shard_map/while/body/eval_jaxpr/sub | solution.py:100
  232.2 4.6 %fusion.122 = f32[4096,128]{1,0:T(8,128)} fusion(bf16[2,128,4096]{2,1,0:T(8,128)(2,1)} %fusion.121, f32[4096,128]{1,0:T(8,128)} %get-tuple-element.308, pred[]{:T(512)S(6)} %compare.5, bf16[4,128,2,128]{3,1,2,0:T(8,128)(2,1)} %get-tuple-element.329, s32[]{:T(128)} %get-tuple-element.307), kind=kOutput, calls=%fused_computation.14.clone.1 | convolution fusion | flops 270008320 | bytes 6357505 | tf_op jit(solution)/shard_map/while/body/eval_jaxpr/hqk,qhd->kd/dot_general | solution.py:112
  243.6 4.9 %fusion.118 = (f32[2,128]{1,0:T(2,128)S(1)}, f32[2,128,4096]{2,1,0:T(8,128)}) fusion(pred[128,4096]{1,0:T(8,128)(4,1)S(1)} %compare_and_fusion.2, bf16[4096,128]{1,0:T(8,128)(2,1)} %get-tuple-element.330, bf16[4,128,2,128]{3,1,2,0:T(8,128)(2,1)} %get-tuple-element.329, s32[]{:T(128)} %get-tuple-element.307), kind=kOutput, calls=%fused_computation.112.clone.1 | convolution fusion | flops 272633856 | bytes 5834240 | tf_op jit(solution)/shard_map/while/body/eval_jaxpr/sub | solution.py:100
  255.1 4.6 %fusion.122 = f32[4096,128]{1,0:T(8,128)} fusion(bf16[2,128,4096]{2,1,0:T(8,128)(2,1)} %fusion.121, f32[4096,128]{1,0:T(8,128)} %get-tuple-element.308, pred[]{:T(512)S(6)} %compare.5, bf16[4,128,2,128]{3,1,2,0:T(8,128)(2,1)} %get-tuple-element.329, s32[]{:T(128)} %get-tuple-element.307), kind=kOutput, calls=%fused_computation.14.clone.1 | convolution fusion | flops 270008320 | bytes 6357505 | tf_op jit(solution)/shard_map/while/body/eval_jaxpr/hqk,qhd->kd/dot_general | solution.py:112
  275.7 3.7 all-to-all-start.2
  281.0 25.1 %all-to-all-done.2 = bf16[8,512,256]{1,2,0:T(8,128)(2,1)S(1)} async-done(((bf16[8,512,256]{1,2,0:T(8,128)(2,1)}), bf16[8,512,256]{1,2,0:T(8,128)(2,1)S(1)}, u32[]{:S(2)}, u32[]{:S(2)}) %all-to-all-start.2) | async-done | bytes 2097184 | tf_op jit(solution)/shard_map/all_to_all | solution.py:54
  309.5 4.5 %add_convert_fusion = bf16[512,4096]{1,0:T(8,128)(2,1)} fusion(f32[512,4096]{1,0:T(8,128)S(1)} %fusion.48, bf16[512,128]{0,1:T(8,128)(2,1)S(1)} %add_convert_fusion.1, bf16[4096,384]{1,0:T(8,128)(2,1)} %all-gather.2.cloned.1.call-done), kind=kOutput, calls=%fused_computation.47 | convolution fusion | flops 541065216 | bytes 13762560 | tf_op jit(solution)/shard_map/dot_general | solution.py:202
  314.2 4.0 convolution_convert_fusion
  318.5 49.5 %all_to_all.20 = bf16[8,512,384]{1,2,0:T(8,128)(2,1)S(1)} all-to-all(bf16[8,512,384]{1,2,0:T(8,128)(2,1)S(1)} %bitcast.185), channel_id=1, replica_groups=mesh['ctx'=8,'tp'=16] {'ctx'}, dimensions={0} | all-to-all | bytes 6291456 | tf_op jit(solution)/shard_map/all_to_all | solution.py:54
  370.4 32.2 %reduce-scatter.2.cloned.1.call-done = bf16[32,4096]{1,0:T(8,128)(2,1)} async-done(((bf16[512,4096]{1,0:T(8,128)(2,1)}), bf16[32,4096]{1,0:T(8,128)(2,1)}) %reduce-scatter.2.cloned.1.call-update) | async-done | bytes 262160 | tf_op jit(solution)/shard_map/reduce_scatter | solution.py:205
  (136 shorter events, 93.3 us)
Async XLA Ops:
  7.2 13.6 %copy-start = (s32[4096]{0:T(1024)S(1)}, s32[4096]{0:T(1024)}, u32[]{:S(2)}) copy-start(s32[4096]{0:T(1024)} %param.13) | copy-start | bytes 49156
  7.2 121.5 %all-gather.2.cloned.1.call-start = ((), (), s32[]{:S(2)}) async-start(), calls=%async_computation.5 | async-start | bytes 3538944 | tf_op jit(solution)/shard_map/all_gather | solution.py:13
  12.5 8.2 %copy-start.13 = (s32[4096]{0:T(1024)S(1)}, s32[4096]{0:T(1024)}, u32[]{:S(2)}) copy-start(s32[4096]{0:T(1024)} %param.12) | copy-start | bytes 49156
  12.5 105.0 %all-to-all-start = ((bf16[16,32,4096]{2,1,0:T(8,128)(2,1)}), bf16[16,32,4096]{2,1,0:T(8,128)(2,1)}, u32[]{:S(2)}, u32[]{:S(2)}) async-start(bf16[16,32,4096]{2,1,0:T(8,128)(2,1)} %stack.2), calls=%async_computation | async-start | bytes 8388608 | tf_op jit(solution)/shard_map/all_to_all | solution.py:137
  132.7 3.8 collective-permute-start
  139.5 4.0 copy-start.14
  139.5 31.7 %all-to-all-start.1 = ((bf16[8,512,256]{1,2,0:T(8,128)(2,1)}), bf16[8,512,256]{1,2,0:T(8,128)(2,1)S(1)}, u32[]{:S(2)}, u32[]{:S(2)}) async-start(bf16[8,512,256]{1,2,0:T(8,128)(2,1)} %broadcast_in_dim.33), calls=%async_computation.1 | async-start | bytes 4194304 | tf_op jit(solution)/shard_map/all_to_all | solution.py:32
  150.3 3.9 copy-start.12
  153.4 20.2 %copy-start.9 = (f32[512,128]{1,0:T(8,128)}, f32[512,128]{1,0:T(8,128)S(1)}, u32[]{:S(2)}) copy-start(f32[512,128]{1,0:T(8,128)S(1)} %copy.70) | copy-start | bytes 786436
  182.1 4.5 %copy-start.3 = (f32[2,128,4096]{2,1,0:T(8,128)S(1)}, f32[2,128,4096]{2,1,0:T(8,128)}, u32[]{:S(2)}) copy-start(f32[2,128,4096]{2,1,0:T(8,128)} %get-tuple-element.291) | copy-start | bytes 12582916 | tf_op jit(solution)/shard_map/while
  188.7 4.0 copy-start.2
  202.8 4.5 %copy-start.3 = (f32[2,128,4096]{2,1,0:T(8,128)S(1)}, f32[2,128,4096]{2,1,0:T(8,128)}, u32[]{:S(2)}) copy-start(f32[2,128,4096]{2,1,0:T(8,128)} %get-tuple-element.291) | copy-start | bytes 12582916 | tf_op jit(solution)/shard_map/while
  209.3 4.6 %copy-start.2 = (bf16[2,128,4096]{2,1,0:T(8,128)(2,1)S(1)}, bf16[2,128,4096]{2,1,0:T(8,128)(2,1)}, u32[]{:S(2)}) copy-start(bf16[2,128,4096]{2,1,0:T(8,128)(2,1)} %fusion.121) | copy-start | bytes 6291460 | tf_op jit(solution)/shard_map/while
  225.6 4.5 %copy-start.3 = (f32[2,128,4096]{2,1,0:T(8,128)S(1)}, f32[2,128,4096]{2,1,0:T(8,128)}, u32[]{:S(2)}) copy-start(f32[2,128,4096]{2,1,0:T(8,128)} %get-tuple-element.291) | copy-start | bytes 12582916 | tf_op jit(solution)/shard_map/while
  232.2 4.6 %copy-start.2 = (bf16[2,128,4096]{2,1,0:T(8,128)(2,1)S(1)}, bf16[2,128,4096]{2,1,0:T(8,128)(2,1)}, u32[]{:S(2)}) copy-start(bf16[2,128,4096]{2,1,0:T(8,128)(2,1)} %fusion.121) | copy-start | bytes 6291460 | tf_op jit(solution)/shard_map/while
  248.5 4.5 %copy-start.3 = (f32[2,128,4096]{2,1,0:T(8,128)S(1)}, f32[2,128,4096]{2,1,0:T(8,128)}, u32[]{:S(2)}) copy-start(f32[2,128,4096]{2,1,0:T(8,128)} %get-tuple-element.291) | copy-start | bytes 12582916 | tf_op jit(solution)/shard_map/while
  255.1 4.6 %copy-start.2 = (bf16[2,128,4096]{2,1,0:T(8,128)(2,1)S(1)}, bf16[2,128,4096]{2,1,0:T(8,128)(2,1)}, u32[]{:S(2)}) copy-start(bf16[2,128,4096]{2,1,0:T(8,128)(2,1)} %fusion.121) | copy-start | bytes 6291460 | tf_op jit(solution)/shard_map/while
  266.0 2.0 copy-start.5
  271.1 1.9 copy-start.8
  275.7 4.0 copy-start.11
  275.7 30.5 %all-to-all-start.2 = ((bf16[8,512,256]{1,2,0:T(8,128)(2,1)}), bf16[8,512,256]{1,2,0:T(8,128)(2,1)S(1)}, u32[]{:S(2)}, u32[]{:S(2)}) async-start(bf16[8,512,256]{1,2,0:T(8,128)(2,1)} %copy.84), calls=%async_computation.2 | async-start | bytes 4194304 | tf_op jit(solution)/shard_map/all_to_all | solution.py:54
  279.4 123.2 %reduce-scatter.2.cloned.1.call-start = ((), (), s32[]{:S(2)}) async-start(), calls=%async_computation.6 | async-start | bytes 4456448 | tf_op jit(solution)/shard_map/reduce_scatter | solution.py:205
  306.5 3.0 collective-permute-start.1
  368.0 34.6 %copy-start.1 = (s32[4096]{0:T(1024)S(1)}, s32[4096]{0:T(1024)}, u32[]{:S(2)}) copy-start(s32[4096]{0:T(1024)} %param.13) | copy-start | bytes 49156
  (4 other events, 5.0 us)
Sparse Core Ops, SparseCore 0:
  10.2 118.4 all-gather.1
  314.2 88.3 reduce-scatter.1
